TPU v7x, 32 devices: a whole 2x2x4 slice. The times are simulated.
32 devices in a mesh: ctx: 8 (over z, x), head: 4 (over y, core).
Axes of the slice: x: 2, y: 2, z: 4, core: 2. Of those that a mesh axis runs over, the one named last changes fastest.
Arguments:
- query: bfloat16 [8, 2, 128, 8192], P('ctx', None, 'head'), may hold values from -200 to 200
- keyval: bfloat16 [8, 2, 2, 128, 1024], P('ctx', None, None, 'head'), may hold values from -6 to 6
- doc_blocks: int32 [4], replicated, may hold values from 1 to 12, 16 in all
Outputs:
- attended: bfloat16 [8, 2, 128, 8192], P('ctx', None, 'head')
Inputs may be any that keep to these rules, and one draw needn't show every extreme that they name: `doc_blocks`: documents fill the sequence in order; the longest has exactly 12 blocks.
All inputs are finite; a program needn't handle non-finite values.
Results may differ from a plain program's by a relative error of at most 0.0038.
Values may be sent and summed in bfloat16 or wider, within the bound.
A program may use at most 64 MiB of HBM per device.

v0:
```python
import jax
import jax.numpy as jnp
from jax import lax
from jax.sharding import PartitionSpec as P

QUERY_HEADS = 64
KEY_VALUE_HEADS = 8
HEAD_WIDTH = 128
BLK = 128


def doc_index(positions, doc_ends):
    return jnp.sum((positions[:, None] >= doc_ends[None, :]).astype(jnp.int32), axis=1)


def local(query, keyval, doc_blocks):
    ctx_count = lax.axis_size("ctx")
    ctx_index = lax.axis_index("ctx")
    span_len = query.shape[2] * lax.axis_size("head")
    width_kv = keyval.shape[4]
    stacked = keyval.reshape(1, 4, keyval.shape[3], width_kv)
    query_heads, kv_heads = (
        lax.all_to_all(query, "head", split_axis=3, concat_axis=2, tiled=True),
        lax.all_to_all(stacked, "head", split_axis=3, concat_axis=2, tiled=True),
    )
    kv_local = kv_heads.shape[3] // HEAD_WIDTH
    heads_per_group = QUERY_HEADS // KEY_VALUE_HEADS
    kv_mine = kv_heads.reshape(1, 2, 2, span_len, kv_local * HEAD_WIDTH)
    row_count = 2 * span_len
    query_rows = query_heads.reshape(row_count, kv_local, heads_per_group, HEAD_WIDTH)
    offsets = jnp.arange(span_len, dtype=jnp.int32)
    query_pos = jnp.concatenate(
        [ctx_index * span_len + offsets, (2 * ctx_count - 1 - ctx_index) * span_len + offsets]
    )
    doc_ends = jnp.cumsum(doc_blocks) * BLK
    query_doc = doc_index(query_pos, doc_ends)
    scale_factor = HEAD_WIDTH ** (-0.5)
    initial = (
        jnp.full((kv_local, heads_per_group, row_count), -1e30, jnp.float32),
        jnp.zeros((kv_local, heads_per_group, row_count), jnp.float32),
        jnp.zeros((row_count, kv_local, heads_per_group, HEAD_WIDTH), jnp.float32),
    )
    gathered = lax.all_gather(kv_mine, "ctx", axis=0, tiled=True)
    running = initial
    count = gathered.shape[0]
    group_size = 4
    group_count = count // group_size
    grouped = gathered.reshape(group_count, group_size, 2, 2, span_len, kv_local * HEAD_WIDTH)
    firsts = jnp.arange(group_count, dtype=jnp.int32) * group_size

    def advance(state, payload):
        block_kv, lead_span = payload
        span_ids = lead_span + jnp.arange(group_size, dtype=jnp.int32)
        lower_pos = span_ids[:, None] * span_len + offsets[None, :]
        upper_pos = (2 * ctx_count - 1 - span_ids)[:, None] * span_len + offsets[None, :]
        key_pos = jnp.stack([lower_pos, upper_pos], axis=1).reshape(-1)
        key_row_block = block_kv[:, 0].reshape(-1, kv_local, HEAD_WIDTH)
        value_rows = block_kv[:, 1].reshape(-1, kv_local, HEAD_WIDTH)
        visible = (query_doc[:, None] == doc_index(key_pos, doc_ends)[None, :]) & (
            key_pos[None, :] <= query_pos[:, None]
        )
        row_max, totals, acc_sum = state
        scores = (
            jnp.einsum(
                "rgjd,kgd->gjrk", query_rows, key_row_block, preferred_element_type=jnp.float32
            )
            * scale_factor
        )
        scores = jnp.where(visible[None, None], scores, -1e30)
        new_max = jnp.maximum(row_max, jnp.max(scores, axis=-1))
        probs = jnp.where(visible[None, None], jnp.exp(scores - new_max[..., None]), 0.0)
        rescale = jnp.exp(row_max - new_max)
        totals = totals * rescale + jnp.sum(probs, axis=-1)
        added = jnp.einsum(
            "gjrk,kgd->rgjd",
            probs.astype(jnp.bfloat16),
            value_rows,
            preferred_element_type=jnp.float32,
        )
        acc_sum = acc_sum * jnp.moveaxis(rescale, 2, 0)[..., None] + added
        state = (new_max, totals, acc_sum)
        return (state, None)

    running, _ = lax.scan(advance, running, (grouped, firsts))
    row_max, totals, acc_sum = running
    result = (acc_sum / jnp.moveaxis(totals, 2, 0)[..., None]).astype(jnp.bfloat16)
    result = result.reshape(1, 2, span_len, kv_local * heads_per_group * HEAD_WIDTH)
    return lax.all_to_all(result, "head", split_axis=2, concat_axis=3, tiled=True)


def solution(mesh):
    placed = (P("ctx", None, "head", None), P("ctx", None, None, "head", None), P())
    return jax.shard_map(
        local, mesh=mesh, in_specs=placed, out_specs=P("ctx", None, "head", None), check_vma=False
    )
```

profile of v0, /device:TPU:0, one launch (start us, length us, event | category | flops | bytes accessed | tf_op | source)
XLA Modules:
  0.0 154.3 jit_solution(14284918072613798459)
XLA Ops:
  6.5 2.2 %copy.50 = bf16[1,2,2,32,1024]{3,2,1,4,0:T(2,128)(2,1)S(1)} copy(bf16[1,2,2,32,1024]{4,3,2,1,0:T(8,128)(2,1)} %param.6) | data formatting | bytes 524288 | tf_op args[1]
  8.8 1.0 reshape.201
  9.7 10.1 %all_to_all.48 = bf16[4,2,16384]{2,1,0:T(2,128)(2,1)S(1)} all-to-all(bf16[4,2,16384]{2,1,0:T(2,128)(2,1)S(1)} %reshape.201), channel_id=1, replica_groups=mesh['ctx'=8,'head'=4] {'head'}, dimensions={0} | all-to-all | bytes 524288 | tf_op jit(solution)/shard_map/all_to_all | solution.py:24
  19.8 0.5 reshape.202
  20.3 0.7 copy.64
  21.0 0.7 copy.52
  21.8 9.2 %copy.53 = bf16[1,2,32,8192]{2,1,0,3:T(2,128)(2,1)} copy(bf16[1,2,32,8192]{3,2,1,0:T(8,128)(2,1)} %param.5) | data formatting | bytes 2097152 | tf_op args[0]
  30.9 6.4 %reshape.203 = bf16[4,2,65536]{2,1,0:T(2,128)(2,1)} reshape(bf16[8192,1,2,32]{3,2,1,0:T(2,128)(2,1)} %bitcast.85) | data formatting | bytes 2097152
  37.3 3.5 %all-to-all-start.1 = ((bf16[4,2,65536]{2,1,0:T(2,128)(2,1)}), bf16[4,2,65536]{2,1,0:T(2,128)(2,1)S(1)}, u32[]{:S(2)}, u32[]{:S(2)}) async-start(bf16[4,2,65536]{2,1,0:T(2,128)(2,1)} %reshape.203), calls=%async_computation.1 | async-start | bytes 2097152 | tf_op jit(solution)/shard_map/all_to_all | solution.py:23
  40.9 0.2 reduce-window.7
  41.1 0.1 convert_reduce_fusion.1
  41.2 14.1 %all-to-all-done.1 = bf16[4,2,65536]{2,1,0:T(2,128)(2,1)S(1)} async-done(((bf16[4,2,65536]{2,1,0:T(2,128)(2,1)}), bf16[4,2,65536]{2,1,0:T(2,128)(2,1)S(1)}, u32[]{:S(2)}, u32[]{:S(2)}) %all-to-all-start.1) | async-done | bytes 1048608 | tf_op jit(solution)/shard_map/all_to_all | solution.py:23
  55.3 3.5 %reshape.204 = bf16[8192,1,2,32]{3,2,1,0:T(2,128)(2,1)} reshape(bf16[4,2,65536]{2,1,0:T(2,128)(2,1)S(1)} %all-to-all-done.1) | data formatting | bytes 2097152
  58.8 9.0 %copy.54 = bf16[1,2,32,4,2048]{4,2,3,1,0:T(8,128)(2,1)S(1)} copy(bf16[1,2,32,4,2048]{2,1,4,3,0:T(2,128)(2,1)} %bitcast.84) | data formatting | bytes 2097152 | tf_op jit(solution)/shard_map/all_to_all | solution.py:23
  67.7 0.2 copy.74
  68.0 0.3 copy.56
  68.3 3.1 %all-gather.2.cloned.1.call-done = bf16[8,2,2,128,256]{4,3,2,1,0:T(8,128)(2,1)} async-done(((bf16[1,2,2,128,256]{4,3,2,1,0:T(8,128)(2,1)}), bf16[8,2,2,128,256]{4,3,2,1,0:T(8,128)(2,1)}) %all-gather.2.cloned.1.call-update) | async-done | bytes 2097168 | tf_op jit(solution)/shard_map/all_gather | solution.py:43
  71.3 52.6 %while.16 = (s32[]{:T(128)}, f32[2,8,256]{2,1,0:T(8,128)S(1)}, f32[2,8,256]{2,1,0:T(8,128)S(1)}, f32[256,2,8,128]{0,3,2,1:T(8,128)}, s32[256]{0:T(256)S(1)}, /*i...) while((s32[]{:T(128)}, f32[2,8,256]{2,1,0:T(8,128)S(1)}, ...), condition=%wide.region_6.7_spmd.clone.clone, body=%wide.region_2.6_spmd.clone.clone.sunk | while | flops 2204406784 | bytes 131365624 | solution.py:84
  71.3 0.6 dynamic_slice.17
  71.9 0.6 subtract_multiply_fusion.2
  72.7 0.1 convert_reduce_fusion.3
  72.8 0.3 compare_and_fusion.2
  73.2 1.3 copy_bitcast_fusion.2
  74.5 0.1 fusion.32
  74.6 0.1 squeeze.23
  74.7 7.2 %fusion.33 = (f32[2,8,256]{2,1,0:T(8,128)S(1)}, f32[2,1024,256,8]{2,1,3,0:T(8,128)}) fusion(pred[256,1024]{0,1:T(8,128)(4,1)S(1)} %compare_and_fusion.2, bf16[256,2,8,128]{3,0,2,1:T(8,128)(2,1)S(1)} %get-tuple-element.319, bf16[1024,2,128,1]{2,1,0,3:T(2,128)(2,1)S(1)} %bitcast.83), kind=kOutput, calls=%fused_computation.3.clone.1 | convolution fusion | flops 1086320640 | bytes 18628608 | tf_op jit(solution)/shard_map/while/body/eval_jaxpr/rgjd,kgd->gjrk/dot_general | solution.py:64
  81.9 0.1 reshape.206
  82.0 9.7 %bitcast_add_fusion.2 = f32[256,2,8,128]{0,3,2,1:T(8,128)} fusion(f32[256,2,8,128]{0,3,2,1:T(8,128)} %get-tuple-element.301, f32[2,1024,256,8]{2,1,3,0:T(8,128)} %get-tuple-element.283, f32[2,8,256]{2,1,0:T(8,128)S(1)} %get-tuple-element.311, pred[256,1024]{0,1:T(8,128)(4,1)S(1)} %compare_and_fusion.2, f32[256,2,8]{0,2,1:T(8,128)S(1)} %get-tuple-element.284, ...), kind=kOutput, calls=%fused_computation.8.clone.1 | convolution fusion | flops 1096286208 | bytes 21790720 | tf_op jit(solution)/shard_map/while/body/eval_jaxpr/gjrk,kgd->rgjd/dot_general | solution.py:74
  91.7 1.6 %copy-done = f32[2,1024,256,8]{2,1,3,0:T(8,128)S(1)} copy-done((f32[2,1024,256,8]{2,1,3,0:T(8,128)S(1)}, f32[2,1024,256,8]{2,1,3,0:T(8,128)}, u32[]{:S(2)}) %copy-start) | copy-done | bytes 16777240 | tf_op jit(solution)/shard_map/while
  93.3 4.0 %fusion.35 = f32[2,8,256]{2,1,0:T(8,128)S(1)} fusion(f32[2,1024,256,8]{2,1,3,0:T(8,128)S(1)} %copy-done, f32[2,8,256]{2,1,0:T(8,128)S(1)} %get-tuple-element.311, pred[256,1024]{0,1:T(8,128)(4,1)S(1)} %compare_and_fusion.2), kind=kLoop, calls=%fused_computation.5.clone.1 | loop fusion | flops 20967424 | bytes 17072128 | tf_op jit(solution)/shard_map/while/body/eval_jaxpr/reduce_sum | solution.py:73
  97.4 0.6 dynamic_slice.17
  97.9 0.6 subtract_multiply_fusion.2
  98.8 0.1 convert_reduce_fusion.3
  98.8 0.3 compare_and_fusion.2
  99.2 1.3 copy_bitcast_fusion.2
  100.5 0.1 fusion.32
  100.6 0.1 squeeze.23
  100.7 7.2 %fusion.33 = (f32[2,8,256]{2,1,0:T(8,128)S(1)}, f32[2,1024,256,8]{2,1,3,0:T(8,128)}) fusion(pred[256,1024]{0,1:T(8,128)(4,1)S(1)} %compare_and_fusion.2, bf16[256,2,8,128]{3,0,2,1:T(8,128)(2,1)S(1)} %get-tuple-element.319, bf16[1024,2,128,1]{2,1,0,3:T(2,128)(2,1)S(1)} %bitcast.83), kind=kOutput, calls=%fused_computation.3.clone.1 | convolution fusion | flops 1086320640 | bytes 18628608 | tf_op jit(solution)/shard_map/while/body/eval_jaxpr/rgjd,kgd->gjrk/dot_general | solution.py:64
  107.9 0.1 reshape.206
  108.1 10.3 %bitcast_add_fusion.2 = f32[256,2,8,128]{0,3,2,1:T(8,128)} fusion(f32[256,2,8,128]{0,3,2,1:T(8,128)} %get-tuple-element.301, f32[2,1024,256,8]{2,1,3,0:T(8,128)} %get-tuple-element.283, f32[2,8,256]{2,1,0:T(8,128)S(1)} %get-tuple-element.311, pred[256,1024]{0,1:T(8,128)(4,1)S(1)} %compare_and_fusion.2, f32[256,2,8]{0,2,1:T(8,128)S(1)} %get-tuple-element.284, ...), kind=kOutput, calls=%fused_computation.8.clone.1 | convolution fusion | flops 1096286208 | bytes 21790720 | tf_op jit(solution)/shard_map/while/body/eval_jaxpr/gjrk,kgd->rgjd/dot_general | solution.py:74
  118.3 1.6 %copy-done = f32[2,1024,256,8]{2,1,3,0:T(8,128)S(1)} copy-done((f32[2,1024,256,8]{2,1,3,0:T(8,128)S(1)}, f32[2,1024,256,8]{2,1,3,0:T(8,128)}, u32[]{:S(2)}) %copy-start) | copy-done | bytes 16777240 | tf_op jit(solution)/shard_map/while
  119.9 4.0 %fusion.35 = f32[2,8,256]{2,1,0:T(8,128)S(1)} fusion(f32[2,1024,256,8]{2,1,3,0:T(8,128)S(1)} %copy-done, f32[2,8,256]{2,1,0:T(8,128)S(1)} %get-tuple-element.311, pred[256,1024]{0,1:T(8,128)(4,1)S(1)} %compare_and_fusion.2), kind=kLoop, calls=%fused_computation.5.clone.1 | loop fusion | flops 20967424 | bytes 17072128 | tf_op jit(solution)/shard_map/while/body/eval_jaxpr/reduce_sum | solution.py:73
  124.0 1.8 %divide_convert_fusion = bf16[256,2,8,128]{0,3,2,1:T(8,128)(2,1)S(1)} fusion(f32[256,2,8,128]{0,3,2,1:T(8,128)} %get-tuple-element.66, f32[256,2,8]{0,2,1:T(8,128)S(1)} %bitcast.97), kind=kLoop, calls=%fused_computation.31 | loop fusion | flops 1048576 | bytes 3162112 | tf_op jit(solution)/shard_map/convert_element_type | solution.py:86
  125.8 0.3 reshape.199
  126.1 3.1 %copy.58 = bf16[1,2,128,2048]{3,1,0,2:T(2,128)(2,1)S(1)} copy(bf16[1,2,128,2048]{2,1,3,0:T(2,128)(2,1)S(1)} %reshape.199) | data formatting | bytes 2097152 | tf_op jit(solution)/shard_map/reshape | solution.py:87
  129.1 17.0 %all_to_all.49 = bf16[1,2,128,2048]{3,1,0,2:T(2,128)(2,1)S(1)} all-to-all(bf16[1,2,128,2048]{3,1,0,2:T(2,128)(2,1)S(1)} %copy.58), channel_id=1, replica_groups=mesh['ctx'=8,'head'=4] {'head'}, dimensions={2} | all-to-all | bytes 2097152 | tf_op jit(solution)/shard_map/all_to_all | solution.py:88
  146.1 0.3 copy.59
  146.5 1.0 copy.73
  (25 shorter events, 0.4 us)
Async XLA Ops:
  6.5 34.4 %copy-start.1 = (s32[4]{0:T(128)S(1)}, s32[4]{0:T(128)}, u32[]{:S(2)}) copy-start(s32[4]{0:T(128)} %param.7) | copy-start | bytes 52
  6.5 64.8 %all-gather.2.cloned.1.call-start = ((), (), s32[]{:S(2)}) async-start(), calls=%async_computation.3 | async-start | bytes 2359296 | tf_op jit(solution)/shard_map/all_gather | solution.py:43
  37.3 17.9 %all-to-all-start.1 = ((bf16[4,2,65536]{2,1,0:T(2,128)(2,1)}), bf16[4,2,65536]{2,1,0:T(2,128)(2,1)S(1)}, u32[]{:S(2)}, u32[]{:S(2)}) async-start(bf16[4,2,65536]{2,1,0:T(2,128)(2,1)} %reshape.203), calls=%async_computation.1 | async-start | bytes 2097152 | tf_op jit(solution)/shard_map/all_to_all | solution.py:23
  82.0 11.3 %copy-start = (f32[2,1024,256,8]{2,1,3,0:T(8,128)S(1)}, f32[2,1024,256,8]{2,1,3,0:T(8,128)}, u32[]{:S(2)}) copy-start(f32[2,1024,256,8]{2,1,3,0:T(8,128)} %get-tuple-element.283) | copy-start | bytes 50331652 | tf_op jit(solution)/shard_map/while
  108.0 11.9 %copy-start = (f32[2,1024,256,8]{2,1,3,0:T(8,128)S(1)}, f32[2,1024,256,8]{2,1,3,0:T(8,128)}, u32[]{:S(2)}) copy-start(f32[2,1024,256,8]{2,1,3,0:T(8,128)} %get-tuple-element.283) | copy-start | bytes 50331652 | tf_op jit(solution)/shard_map/while
Sparse Core Ops, SparseCore 0:
  21.9 49.4 all-gather.1
where the time goes:
time: 156 us; the launch traced here: 154 us
  local copies, waits for them, and re-layouts  46 us (29%)
  matrix products  34.3 us (22%)
  blocking collectives  27 us (17%)
  waiting for transfers between devices  17.2 us (11%)
  between operations  13.5 us (9%)
  other arithmetic  12.5 us (8%)
  starting transfers between devices  3.52 us (2%)
    unnamed x10, local copies, waits for them, and re-layouts  23.3 us
    dot_general x2, matrix products, advance(): jnp.einsum('gjrk,kgd->rgjd', probs.astype(jnp.bfloat16), value_rows, pref...  20 us
    all_to_all x1, blocking collectives, local(): lax.all_to_all(result, 'head', split_axis=2, concat_axis=3, tiled=True)  17 us
    dot_general x2, matrix products, advance(): jnp.einsum('rgjd,kgd->gjrk', query_rows, key_row_block, preferred_element...  14.3 us
    all_to_all x1, waiting for transfers between devices, local(): lax.all_to_all(query, 'head', split_axis=3, concat_axis=2, tiled=True)  14.1 us
    all_to_all x1, blocking collectives, local(): lax.all_to_all(stacked, 'head', split_axis=3, concat_axis=2, tiled=True)  10.1 us
    all_to_all x1, local copies, waits for them, and re-layouts, local(): lax.all_to_all(query, 'head', split_axis=3, concat_axis=2, tiled=True)  8.96 us
    reduce_sum x2, other arithmetic, advance(): totals = totals * rescale + jnp.sum(probs, axis=-1)  7.97 us
  transfers between devices with their start and end apart: 2, of which 2 were waited for; matrix products, arithmetic and copies ran while one was open for 19% of the time, Pallas kernels for 0%

commit v1 on v0

--- a/solution.py
+++ b/solution.py
@@ -7,6 +7,22 @@
 KEY_VALUE_HEADS = 8
 HEAD_WIDTH = 128
 BLK = 128
+
+
+def pairwise_exchange(array, axis, split, join):
+    ways, here = (lax.axis_size(axis), lax.axis_index(axis))
+    width = array.shape[split] // ways
+    lengths = list(array.shape)
+    lengths[split] = width
+    height = lengths[join]
+    lengths[join] = height * ways
+    full = jnp.zeros(lengths, array.dtype)
+    for mask in range(ways):
+        part = lax.dynamic_slice_in_dim(array, (here ^ mask) * width, width, axis=split)
+        if mask:
+            part = lax.ppermute(part, axis, [(d, d ^ mask) for d in range(ways)])
+        full = lax.dynamic_update_slice_in_dim(full, part, (here ^ mask) * height, axis=join)
+    return full
 
 
 def doc_index(positions, doc_ends):
@@ -21,7 +37,7 @@
     stacked = keyval.reshape(1, 4, keyval.shape[3], width_kv)
     query_heads, kv_heads = (
         lax.all_to_all(query, "head", split_axis=3, concat_axis=2, tiled=True),
-        lax.all_to_all(stacked, "head", split_axis=3, concat_axis=2, tiled=True),
+        pairwise_exchange(stacked, "head", 3, 2),
     )
     kv_local = kv_heads.shape[3] // HEAD_WIDTH
     heads_per_group = QUERY_HEADS // KEY_VALUE_HEADS

time: 156 us -> 150 us (0.962)
  blocking collectives: 27 us -> 17 us
  waiting for transfers between devices: 17.2 us -> 21.1 us
  local copies, waits for them, and re-layouts: 46 us -> 42.7 us
  starting transfers between devices: 3.52 us -> 6.7 us
    all_to_all x1 -> x0, blocking collectives: 10.1 us -> none  [local(): lax.all_to_all(stacked, 'head', split_axis=3, concat_axis=2, tiled=True)]
    ppermute x0 -> x3, waiting for transfers between devices: none -> 3.99 us  [pairwise_exchange(): part = lax.ppermute(part, axis, [(d, d ^ mask) for d in range(ways)])]
    ppermute x0 -> x3, starting transfers between devices: none -> 3.18 us  [pairwise_exchange(): part = lax.ppermute(part, axis, [(d, d ^ mask) for d in range(ways)])]
    unnamed x10 -> x7, local copies, waits for them, and re-layouts: 23.3 us -> 20.3 us
  transfers between devices with their start and end apart: 2 -> 5, of which waited for: 2 -> 4; matrix products, arithmetic and copies ran while one was open for 19% -> 20% of each run, Pallas kernels for 0% -> 0%
where the time goes in v1:
time: 150 us; the launch traced here: 149 us
  local copies, waits for them, and re-layouts  42.7 us (28%)
  matrix products  34.3 us (23%)
  waiting for transfers between devices  21.1 us (14%)
  blocking collectives  17 us (11%)
  between operations  13.5 us (9%)
  other arithmetic  13.2 us (9%)
  starting transfers between devices  6.7 us (4%)
    unnamed x7, local copies, waits for them, and re-layouts  20.3 us
    dot_general x2, matrix products, advance(): jnp.einsum('gjrk,kgd->rgjd', probs.astype(jnp.bfloat16), value_rows, pref...  20 us
    all_to_all x1, blocking collectives, local(): lax.all_to_all(result, 'head', split_axis=2, concat_axis=3, tiled=True)  17 us
    dot_general x2, matrix products, advance(): jnp.einsum('rgjd,kgd->gjrk', query_rows, key_row_block, preferred_element...  14.3 us
    all_to_all x1, waiting for transfers between devices, local(): lax.all_to_all(query, 'head', split_axis=3, concat_axis=2, tiled=True)  13.4 us
    all_to_all x1, local copies, waits for them, and re-layouts, local(): lax.all_to_all(query, 'head', split_axis=3, concat_axis=2, tiled=True)  8.97 us
    reduce_sum x2, other arithmetic, advance(): totals = totals * rescale + jnp.sum(probs, axis=-1)  7.97 us
    ppermute x3, waiting for transfers between devices, pairwise_exchange(): part = lax.ppermute(part, axis, [(d, d ^ mask) for d in range(ways)])  3.99 us
  transfers between devices with their start and end apart: 5, of which 4 were waited for; matrix products, arithmetic and copies ran while one was open for 20% of the time, Pallas kernels for 0%

profile of v1, /device:TPU:0, one launch (start us, length us, event | category | flops | bytes accessed | tf_op | source)
XLA Modules:
  0.0 148.7 jit_solution(17407078603949474080)
XLA Ops:
  6.6 1.0 constant_dynamic-slice_fusion.1
  7.5 0.6 collective-permute-start
  8.1 2.6 %collective-permute-start.1 = (bf16[1,4,32,256]{3,2,1,0:T(8,128)(2,1)S(1)}, bf16[1,4,32,256]{3,2,1,0:T(8,128)(2,1)S(1)}, u32[]{:S(2)}, u32[]{:S(2)}) collective-permute-start(bf16[1,4,32,256]{3,2,1,0:T(8,128)(2,1)S(1)} %get-tuple-element.208), channel_id=1, source_target_pairs={{0,2},{1,3},{2,0},{3,1},{4,6},{5,7},{6,4},{7,5},{8,10},{9,11},{10,... | collective-permute-start | bytes 196616 | tf_op jit(solution)/shard_map/ppermute | solution.py:23
  10.7 2.6 %collective-permute-done.1 = bf16[1,4,32,256]{3,2,1,0:T(8,128)(2,1)S(1)} collective-permute-done((bf16[1,4,32,256]{3,2,1,0:T(8,128)(2,1)S(1)}, bf16[1,4,32,256]{3,2,1,0:T(8,128)(2,1)S(1)}, u32[]{:S(2)}, u32[]{:S(2)}) %collective-permute-start.1) | collective-permute-done | bytes 65568 | tf_op jit(solution)/shard_map/ppermute | solution.py:23
  13.4 1.4 collective-permute-done.2
  14.8 0.7 copy-done.1
  15.5 9.2 %copy.43 = bf16[1,2,32,8192]{2,1,0,3:T(2,128)(2,1)} copy(bf16[1,2,32,8192]{3,2,1,0:T(8,128)(2,1)} %param.5) | data formatting | bytes 2097152 | tf_op args[0]
  24.6 6.5 %reshape.200 = bf16[4,2,65536]{2,1,0:T(2,128)(2,1)} reshape(bf16[8192,1,2,32]{3,2,1,0:T(2,128)(2,1)} %bitcast.81) | data formatting | bytes 2097152
  31.1 3.5 %all-to-all-start = ((bf16[4,2,65536]{2,1,0:T(2,128)(2,1)}), bf16[4,2,65536]{2,1,0:T(2,128)(2,1)S(1)}, u32[]{:S(2)}, u32[]{:S(2)}) async-start(bf16[4,2,65536]{2,1,0:T(2,128)(2,1)} %reshape.200), calls=%async_computation | async-start | bytes 2097152 | tf_op jit(solution)/shard_map/all_to_all | solution.py:39
  34.7 0.8 reduce-window.7
  35.5 0.1 convert_reduce_fusion.1
  35.6 13.4 %all-to-all-done = bf16[4,2,65536]{2,1,0:T(2,128)(2,1)S(1)} async-done(((bf16[4,2,65536]{2,1,0:T(2,128)(2,1)}), bf16[4,2,65536]{2,1,0:T(2,128)(2,1)S(1)}, u32[]{:S(2)}, u32[]{:S(2)}) %all-to-all-start) | async-done | bytes 1048608 | tf_op jit(solution)/shard_map/all_to_all | solution.py:39
  49.0 3.5 %reshape.201 = bf16[8192,1,2,32]{3,2,1,0:T(2,128)(2,1)} reshape(bf16[4,2,65536]{2,1,0:T(2,128)(2,1)S(1)} %all-to-all-done) | data formatting | bytes 2097152
  52.5 9.0 %copy.44 = bf16[1,2,32,4,2048]{4,2,3,1,0:T(8,128)(2,1)S(1)} copy(bf16[1,2,32,4,2048]{2,1,4,3,0:T(2,128)(2,1)} %bitcast.80) | data formatting | bytes 2097152 | tf_op jit(solution)/shard_map/all_to_all | solution.py:39
  61.5 0.2 copy.63
  61.8 0.3 copy.46
  62.0 3.6 %all-gather.2.cloned.1.call-done = bf16[8,2,2,128,256]{4,3,2,1,0:T(8,128)(2,1)} async-done(((bf16[1,2,2,128,256]{4,3,2,1,0:T(8,128)(2,1)}), bf16[8,2,2,128,256]{4,3,2,1,0:T(8,128)(2,1)}) %all-gather.2.cloned.1.call-update) | async-done | bytes 2097168 | tf_op jit(solution)/shard_map/all_gather | solution.py:59
  65.7 52.6 %while.16 = (s32[]{:T(128)}, f32[2,8,256]{2,1,0:T(8,128)S(1)}, f32[2,8,256]{2,1,0:T(8,128)S(1)}, f32[256,2,8,128]{0,3,2,1:T(8,128)}, s32[256]{0:T(256)S(1)}, /*i...) while((s32[]{:T(128)}, f32[2,8,256]{2,1,0:T(8,128)S(1)}, ...), condition=%wide.region_6.7_spmd.clone.clone, body=%wide.region_2.6_spmd.clone.clone.sunk | while | flops 2204406784 | bytes 131365624 | solution.py:100
  65.7 0.6 dynamic_slice.37
  66.3 0.6 subtract_multiply_fusion.2
  67.1 0.1 convert_reduce_fusion.3
  67.2 0.3 compare_and_fusion.2
  67.5 1.3 copy_bitcast_fusion.2
  68.8 0.1 fusion.32
  68.9 0.1 squeeze.23
  69.0 7.2 %fusion.33 = (f32[2,8,256]{2,1,0:T(8,128)S(1)}, f32[2,1024,256,8]{2,1,3,0:T(8,128)}) fusion(pred[256,1024]{0,1:T(8,128)(4,1)S(1)} %compare_and_fusion.2, bf16[256,2,8,128]{3,0,2,1:T(8,128)(2,1)S(1)} %get-tuple-element.323, bf16[1024,2,128,1]{2,1,0,3:T(2,128)(2,1)S(1)} %bitcast.79), kind=kOutput, calls=%fused_computation.3.clone.1 | convolution fusion | flops 1086320640 | bytes 18628608 | tf_op jit(solution)/shard_map/while/body/eval_jaxpr/rgjd,kgd->gjrk/dot_general | solution.py:80
  76.2 0.1 reshape.203
  76.4 9.7 %bitcast_add_fusion.2 = f32[256,2,8,128]{0,3,2,1:T(8,128)} fusion(f32[256,2,8,128]{0,3,2,1:T(8,128)} %get-tuple-element.305, f32[2,1024,256,8]{2,1,3,0:T(8,128)} %get-tuple-element.287, f32[2,8,256]{2,1,0:T(8,128)S(1)} %get-tuple-element.315, pred[256,1024]{0,1:T(8,128)(4,1)S(1)} %compare_and_fusion.2, f32[256,2,8]{0,2,1:T(8,128)S(1)} %get-tuple-element.288, ...), kind=kOutput, calls=%fused_computation.8.clone.1 | convolution fusion | flops 1096286208 | bytes 21790720 | tf_op jit(solution)/shard_map/while/body/eval_jaxpr/gjrk,kgd->rgjd/dot_general | solution.py:90
  86.1 1.6 %copy-done = f32[2,1024,256,8]{2,1,3,0:T(8,128)S(1)} copy-done((f32[2,1024,256,8]{2,1,3,0:T(8,128)S(1)}, f32[2,1024,256,8]{2,1,3,0:T(8,128)}, u32[]{:S(2)}) %copy-start) | copy-done | bytes 16777240 | tf_op jit(solution)/shard_map/while
  87.6 4.0 %fusion.35 = f32[2,8,256]{2,1,0:T(8,128)S(1)} fusion(f32[2,1024,256,8]{2,1,3,0:T(8,128)S(1)} %copy-done, f32[2,8,256]{2,1,0:T(8,128)S(1)} %get-tuple-element.315, pred[256,1024]{0,1:T(8,128)(4,1)S(1)} %compare_and_fusion.2), kind=kLoop, calls=%fused_computation.5.clone.1 | loop fusion | flops 20967424 | bytes 17072128 | tf_op jit(solution)/shard_map/while/body/eval_jaxpr/reduce_sum | solution.py:89
  91.7 0.6 dynamic_slice.37
  92.3 0.6 subtract_multiply_fusion.2
  93.1 0.1 convert_reduce_fusion.3
  93.2 0.3 compare_and_fusion.2
  93.5 1.3 copy_bitcast_fusion.2
  94.8 0.1 fusion.32
  94.9 0.1 squeeze.23
  95.1 7.2 %fusion.33 = (f32[2,8,256]{2,1,0:T(8,128)S(1)}, f32[2,1024,256,8]{2,1,3,0:T(8,128)}) fusion(pred[256,1024]{0,1:T(8,128)(4,1)S(1)} %compare_and_fusion.2, bf16[256,2,8,128]{3,0,2,1:T(8,128)(2,1)S(1)} %get-tuple-element.323, bf16[1024,2,128,1]{2,1,0,3:T(2,128)(2,1)S(1)} %bitcast.79), kind=kOutput, calls=%fused_computation.3.clone.1 | convolution fusion | flops 1086320640 | bytes 18628608 | tf_op jit(solution)/shard_map/while/body/eval_jaxpr/rgjd,kgd->gjrk/dot_general | solution.py:80
  102.2 0.1 reshape.203
  102.4 10.3 %bitcast_add_fusion.2 = f32[256,2,8,128]{0,3,2,1:T(8,128)} fusion(f32[256,2,8,128]{0,3,2,1:T(8,128)} %get-tuple-element.305, f32[2,1024,256,8]{2,1,3,0:T(8,128)} %get-tuple-element.287, f32[2,8,256]{2,1,0:T(8,128)S(1)} %get-tuple-element.315, pred[256,1024]{0,1:T(8,128)(4,1)S(1)} %compare_and_fusion.2, f32[256,2,8]{0,2,1:T(8,128)S(1)} %get-tuple-element.288, ...), kind=kOutput, calls=%fused_computation.8.clone.1 | convolution fusion | flops 1096286208 | bytes 21790720 | tf_op jit(solution)/shard_map/while/body/eval_jaxpr/gjrk,kgd->rgjd/dot_general | solution.py:90
  112.7 1.6 %copy-done = f32[2,1024,256,8]{2,1,3,0:T(8,128)S(1)} copy-done((f32[2,1024,256,8]{2,1,3,0:T(8,128)S(1)}, f32[2,1024,256,8]{2,1,3,0:T(8,128)}, u32[]{:S(2)}) %copy-start) | copy-done | bytes 16777240 | tf_op jit(solution)/shard_map/while
  114.2 4.0 %fusion.35 = f32[2,8,256]{2,1,0:T(8,128)S(1)} fusion(f32[2,1024,256,8]{2,1,3,0:T(8,128)S(1)} %copy-done, f32[2,8,256]{2,1,0:T(8,128)S(1)} %get-tuple-element.315, pred[256,1024]{0,1:T(8,128)(4,1)S(1)} %compare_and_fusion.2), kind=kLoop, calls=%fused_computation.5.clone.1 | loop fusion | flops 20967424 | bytes 17072128 | tf_op jit(solution)/shard_map/while/body/eval_jaxpr/reduce_sum | solution.py:89
  118.3 1.8 %divide_convert_fusion = bf16[256,2,8,128]{0,3,2,1:T(8,128)(2,1)S(1)} fusion(f32[256,2,8,128]{0,3,2,1:T(8,128)} %get-tuple-element.66, f32[256,2,8]{0,2,1:T(8,128)S(1)} %bitcast.90), kind=kLoop, calls=%fused_computation.31 | loop fusion | flops 1048576 | bytes 3162112 | tf_op jit(solution)/shard_map/convert_element_type | solution.py:102
  120.1 0.3 reshape.198
  120.4 3.1 %copy.48 = bf16[1,2,128,2048]{3,1,0,2:T(2,128)(2,1)S(1)} copy(bf16[1,2,128,2048]{2,1,3,0:T(2,128)(2,1)S(1)} %reshape.198) | data formatting | bytes 2097152 | tf_op jit(solution)/shard_map/reshape | solution.py:103
  123.4 17.0 %all_to_all.33 = bf16[1,2,128,2048]{3,1,0,2:T(2,128)(2,1)S(1)} all-to-all(bf16[1,2,128,2048]{3,1,0,2:T(2,128)(2,1)S(1)} %copy.48), channel_id=1, replica_groups=mesh['ctx'=8,'head'=4] {'head'}, dimensions={2} | all-to-all | bytes 2097152 | tf_op jit(solution)/shard_map/all_to_all | solution.py:104
  140.4 0.3 copy.49
  140.8 1.0 copy.62
  (30 shorter events, 0.5 us)
Async XLA Ops:
  6.5 59.1 %all-gather.2.cloned.1.call-start = ((), (), s32[]{:S(2)}) async-start(), calls=%async_computation.2 | async-start | bytes 2359296 | tf_op jit(solution)/shard_map/all_gather | solution.py:59
  7.5 3.2 %collective-permute-start = (bf16[1,4,32,256]{3,2,1,0:T(8,128)(2,1)S(1)}, bf16[1,4,32,256]{3,2,1,0:T(8,128)(2,1)S(1)}, u32[]{:S(2)}, u32[]{:S(2)}) collective-permute-start(bf16[1,4,32,256]{3,2,1,0:T(8,128)(2,1)S(1)} %get-tuple-element.209), channel_id=1, source_target_pairs={{0,1},{1,0},{2,3},{3,2},{4,5},{5,4},{6,7},{7,6},{8,9},{9,8},{10,11... | collective-permute-start | bytes 196616 | tf_op jit(solution)/shard_map/ppermute | solution.py:23
  8.1 5.3 %collective-permute-start.1 = (bf16[1,4,32,256]{3,2,1,0:T(8,128)(2,1)S(1)}, bf16[1,4,32,256]{3,2,1,0:T(8,128)(2,1)S(1)}, u32[]{:S(2)}, u32[]{:S(2)}) collective-permute-start(bf16[1,4,32,256]{3,2,1,0:T(8,128)(2,1)S(1)} %get-tuple-element.208), channel_id=1, source_target_pairs={{0,2},{1,3},{2,0},{3,1},{4,6},{5,7},{6,4},{7,5},{8,10},{9,11},{10,... | collective-permute-start | bytes 196616 | tf_op jit(solution)/shard_map/ppermute | solution.py:23
  10.7 4.1 %collective-permute-start.2 = (bf16[1,4,32,256]{3,2,1,0:T(8,128)(2,1)S(1)}, bf16[1,4,32,256]{3,2,1,0:T(8,128)(2,1)S(1)}, u32[]{:S(2)}, u32[]{:S(2)}) collective-permute-start(bf16[1,4,32,256]{3,2,1,0:T(8,128)(2,1)S(1)} %get-tuple-element.207), channel_id=1, source_target_pairs={{0,3},{1,2},{2,1},{3,0},{4,7},{5,6},{6,5},{7,4},{8,11},{9,10},{10,... | collective-permute-start | bytes 196616 | tf_op jit(solution)/shard_map/ppermute | solution.py:23
  14.7 0.7 copy-start.1
  31.1 17.9 %all-to-all-start = ((bf16[4,2,65536]{2,1,0:T(2,128)(2,1)}), bf16[4,2,65536]{2,1,0:T(2,128)(2,1)S(1)}, u32[]{:S(2)}, u32[]{:S(2)}) async-start(bf16[4,2,65536]{2,1,0:T(2,128)(2,1)} %reshape.200), calls=%async_computation | async-start | bytes 2097152 | tf_op jit(solution)/shard_map/all_to_all | solution.py:39
  76.3 11.3 %copy-start = (f32[2,1024,256,8]{2,1,3,0:T(8,128)S(1)}, f32[2,1024,256,8]{2,1,3,0:T(8,128)}, u32[]{:S(2)}) copy-start(f32[2,1024,256,8]{2,1,3,0:T(8,128)} %get-tuple-element.287) | copy-start | bytes 50331652 | tf_op jit(solution)/shard_map/while
  102.4 11.9 %copy-start = (f32[2,1024,256,8]{2,1,3,0:T(8,128)S(1)}, f32[2,1024,256,8]{2,1,3,0:T(8,128)}, u32[]{:S(2)}) copy-start(f32[2,1024,256,8]{2,1,3,0:T(8,128)} %get-tuple-element.287) | copy-start | bytes 50331652 | tf_op jit(solution)/shard_map/while
Sparse Core Ops, SparseCore 0:
  15.6 50.0 all-gather.1
